TPU v7x, 128 devices: a whole 4x4x4 slice. The times are simulated.
128 devices in a mesh: dp: 32 (over x, z, core), rep: 4 (over y).
Axes of the slice: x: 4, y: 4, z: 4, core: 2. Of those that a mesh axis runs over, the one named last changes fastest.
Arguments:
- cross_in: bfloat16 [65536, 3456], P(('dp', 'rep')), may hold values from -24 to 24
- cotangent: bfloat16 [65536, 3456], P(('dp', 'rep')), may hold values from -24 to 24
- weight_down: bfloat16 [3456, 512], replicated, may hold values from -0.109375 to 0.109375
- weight_up: bfloat16 [512, 3456], replicated, may hold values from -0.25 to 0.25
- cross_bias: float32 [3456], replicated, may hold values from -3 to 3
- row_place: int32 [65536, 26], P(('dp', 'rep')), may hold values from 0 to 66559, as said below
- frequent_table: float32 [1024, 128], replicated, may hold values from -0.6 to 0.6
- frequent_accum: float32 [1024], replicated, may hold values from 416 to 106496
- shard_table: float32 [65536, 128], P('dp'), may hold values from -0.6 to 0.6
- shard_accum: float32 [65536], P('dp'), may hold values from 0.01 to 1
Outputs:
- new_frequent: float32 [1024, 128], replicated
- new_frequent_accum: float32 [1024], replicated
- new_shard: float32 [65536, 128], P('dp')
- new_shard_accum: float32 [65536], P('dp')
- grad_up: float32 [512, 3456], P(('dp', 'rep'))
- grad_down: float32 [3456, 512], P(('dp', 'rep'))
- grad_bias: float32 [3456], P(('dp', 'rep'))
Inputs may be any that keep to these rules, and one draw needn't show every extreme that they name: `row_place`: within the rows of one device (aligned blocks of 512 samples), at most 208 entries name rows of any one owner, and in every block some owner is named by exactly 208 entries; every owner is named at least once in every block.
All inputs are finite; a program needn't handle non-finite values.
Results may differ from a plain program's by a relative error of at most 0.0013.
The roundings to bfloat16 on the way count: a program that leaves them out, or rounds other values in their place, can miss the bound.
Values sent between devices are 32-bit elements; how exact they have to be, the bound alone decides.
A program may use at most 192 MiB of HBM per device.

v0:
```python
import jax
import jax.numpy as jnp
from jax import lax
from jax.sharding import PartitionSpec as P

learn_rate = 0.05
eps_ada = 1e-08


def row_adagrad(table, accum, grad):
    accum_new = accum + jnp.mean(grad * grad, axis=1)
    return (table - learn_rate * grad / (jnp.sqrt(accum_new)[:, None] + eps_ada), accum_new)


def body(
    cross_in,
    cotangent,
    weight_down,
    weight_up,
    cross_bias,
    row_place,
    frequent_table,
    frequent_accum,
    shard_table,
    shard_accum,
):
    emb_width = frequent_table.shape[1]
    num_tables = row_place.shape[1]
    local_rows = cross_in.shape[0]
    f_count = frequent_table.shape[0]
    owned_rows = shard_table.shape[0]
    hidden = jnp.dot(cross_in, weight_down, preferred_element_type=jnp.float32).astype(jnp.bfloat16)
    scaled = jnp.dot(hidden, weight_up, preferred_element_type=jnp.float32) + cross_bias
    cot_wide = cotangent.astype(jnp.float32)
    inner = cot_wide * cross_in.astype(jnp.float32)
    inner_half = inner.astype(jnp.bfloat16)
    back_low = lax.dot_general(
        inner_half, weight_up, (((1,), (1,)), ((), ())), preferred_element_type=jnp.float32
    ).astype(jnp.bfloat16)
    back_in = cot_wide * (scaled + 1.0) + lax.dot_general(
        back_low, weight_down, (((1,), (1,)), ((), ())), preferred_element_type=jnp.float32
    )
    local_up = lax.dot_general(
        hidden, inner_half, (((0,), (0,)), ((), ())), preferred_element_type=jnp.float32
    )
    local_down = lax.dot_general(
        cross_in, back_low, (((0,), (0,)), ((), ())), preferred_element_type=jnp.float32
    )
    local_bias = jnp.sum(inner, axis=0)
    grad_up, grad_down, grad_bias = (
        lax.psum_scatter(local_up, ("dp", "rep"), scatter_dimension=0, tiled=True),
        lax.psum_scatter(local_down, ("dp", "rep"), scatter_dimension=0, tiled=True),
        lax.psum_scatter(local_bias, ("dp", "rep"), scatter_dimension=0, tiled=True),
    )
    values = back_in[:, emb_width:].reshape(local_rows * num_tables, emb_width)
    places = row_place.reshape(-1)
    is_frequent = places < f_count
    freq_grad = jax.ops.segment_sum(values, jnp.where(is_frequent, places, f_count), f_count + 1)[
        :f_count
    ]
    shards = lax.axis_size("dp")
    capacity = local_rows * num_tables // (2 * shards)
    owners = jnp.where(is_frequent, shards, (places - f_count) // owned_rows)
    owner_row = jnp.where(is_frequent, 0, (places - f_count) % owned_rows)
    sorted_order = jnp.argsort(owners, stable=True)
    sorted_owner = owners[sorted_order]
    counts = jnp.sum((owners[:, None] == jnp.arange(shards + 1)[None, :]).astype(jnp.int32), axis=0)
    starts = jnp.cumsum(counts) - counts
    slot_pos = jnp.arange(owners.shape[0]) - starts[sorted_owner]
    target = jnp.where(sorted_owner < shards, sorted_owner * capacity + slot_pos, shards * capacity)
    bucket = (
        jnp.zeros((shards * capacity + 1, emb_width), jnp.float32)
        .at[target]
        .set(values[sorted_order])
    )
    bucket = bucket[: shards * capacity].reshape(shards, capacity, emb_width)
    bucket_rows = (
        jnp.zeros((shards * capacity + 1,), jnp.int32).at[target].set(owner_row[sorted_order])
    )
    bucket_rows = bucket_rows[: shards * capacity].reshape(shards, capacity)
    arrived, arrived_rows = (
        lax.all_to_all(bucket, "dp", split_axis=0, concat_axis=0, tiled=True),
        lax.all_to_all(bucket_rows, "dp", split_axis=0, concat_axis=0, tiled=True),
    )
    shard_grad = jax.ops.segment_sum(
        arrived.reshape(-1, emb_width), arrived_rows.reshape(-1), owned_rows
    )
    shard_grad = lax.psum(shard_grad, "rep")
    new_shard, new_shard_accum = row_adagrad(shard_table, shard_accum, shard_grad)
    freq_total = lax.psum(freq_grad, ("dp", "rep"))
    new_frequent, new_frequent_accum = row_adagrad(frequent_table, frequent_accum, freq_total)
    return (
        new_frequent,
        new_frequent_accum,
        new_shard,
        new_shard_accum,
        grad_up,
        grad_down,
        grad_bias,
    )


def solution(mesh):
    in_specs = (
        P(("dp", "rep"), None),
        P(("dp", "rep"), None),
        P(),
        P(),
        P(),
        P(("dp", "rep"), None),
        P(),
        P(),
        P("dp", None),
        P("dp"),
    )
    out_specs = (
        P(),
        P(),
        P("dp", None),
        P("dp"),
        P(("dp", "rep"), None),
        P(("dp", "rep"), None),
        P(("dp", "rep")),
    )
    return jax.shard_map(body, mesh=mesh, in_specs=in_specs, out_specs=out_specs, check_vma=False)
```

profile of v0, /device:TPU:1, one launch (start us, length us, event | category | flops | bytes accessed | tf_op | source)
XLA Modules:
  0.0 876.3 jit_solution(13880018079292635862)
XLA Ops:
  22.4 9.1 %sort.17 = (s32[13312]{0:T(1024)}, s32[13312]{0:T(1024)}) sort(s32[13312]{0:T(1024)} %copy-done.2, s32[13312]{0:T(1024)} %iota.12), dimensions={0}, to_apply=%region_3.0 | sort | flops 186368 | bytes 212992 | tf_op jit(solution)/shard_map/jit(argsort)/sort | solution.py:65
  32.9 121.2 %gather_fusion = s32[13312]{0:T(1024)} fusion(s32[13312]{0:T(1024)} %copy-done.2, s32[13312]{0:T(1024)} %fusion.19), kind=kCustom, calls=%fused_computation | custom fusion | bytes 159744 | tf_op jit(solution)/shard_map/gather | solution.py:66
  154.1 5.3 compare_select_fusion.3
  159.4 4.2 compare_reduce_fusion.25
  163.7 16.6 %select_select_fusion = s32[13312]{0:T(1024)S(1)} fusion(pred[13312]{0:T(1024)(128)(4,1)S(1)} %get-tuple-element.62, pred[13312]{0:T(1024)(128)(4,1)S(1)} %get-tuple-element.61, pred[13312]{0:T(1024)(128)(4,1)S(1)} %get-tuple-element.60, pred[13312]{0:T(1024)(128)(4,1)S(1)} %get-tuple-element.59, pred[13312]{0:T(1024)(128)(4,1)S(1)} %get-tuple-element.58, ...), kind=kLoop, calls=%fused_computation.77 | loop fusion | flops 346112 | bytes 452712 | tf_op jit(solution)/shard_map/gather | solution.py:69
  181.8 120.7 %gather_fusion.1 = s32[13312]{0:T(1024)} fusion(s32[13312]{0:T(1024)} %get-tuple-element.72, s32[13312]{0:T(1024)} %fusion.19), kind=kCustom, calls=%fused_computation.1 | custom fusion | bytes 159744 | tf_op jit(solution)/shard_map/gather | solution.py:78
  302.6 49.8 %scatter_custom_fusion.1 = s32[6657]{0:T(1024)} fusion(s32[13312]{0:T(1024)} %bitcast.62, s32[13312]{0:T(1024)} %gather_fusion.1, s32[]{:T(128)} %constant.29.clone.1), kind=kCustom, calls=%fused_computation.83 | custom fusion | bytes 27140 | tf_op jit(solution)/shard_map/scatter | solution.py:78
  353.9 9.8 %all-to-all-start = ((s32[32,1,208]{2,1,0:T(1,128)}), s32[32,1,208]{2,1,0:T(1,128)}, u32[]{:S(2)}, u32[]{:S(2)}) async-start(s32[32,1,208]{2,1,0:T(1,128)} %all_to_all.9), calls=%async_computation | async-start | bytes 65536 | tf_op jit(solution)/shard_map/all_to_all | solution.py:83
  363.7 2.6 convert_element_type.18
  369.9 2.1 fusion.10
  374.3 2.1 fusion.27
  376.4 3.3 slice_add_fusion
  379.7 7.8 reshape.231
  387.5 108.6 %scatter_custom_fusion.2 = f32[6657,128]{1,0:T(8,128)S(1)} fusion(s32[13312]{0:T(1024)} %bitcast.63, f32[13312,128]{1,0:T(8,128)} %reshape.231, s32[13312]{0:T(1024)} %fusion.19, f32[]{:T(128)} %constant.21.clone.1), kind=kCustom, calls=%fused_computation.12 | custom fusion | bytes 3408896 | tf_op jit(solution)/shard_map/scatter | solution.py:74
  498.2 7.8 all-to-all-start.1
  511.1 72.4 %scatter_custom_fusion = f32[1025,128]{1,0:T(8,128)} fusion(s32[13312]{0:T(1024)} %bitcast.64, f32[13312,128]{1,0:T(8,128)} %reshape.231, f32[]{:T(128)} %constant.21.clone.1), kind=kCustom, calls=%fused_computation.33 | custom fusion | flops 1703936 | bytes 525312 | tf_op jit(solution)/shard_map/scatter-add | solution.py:58
  588.2 41.0 %scatter_custom_fusion.3 = f32[2048,128]{1,0:T(8,128)} fusion(s32[6656]{0:T(1024)} %reshape.253, f32[6656,128]{1,0:T(8,128)} %bitcast.40, f32[]{:T(128)} %constant.21.clone.1), kind=kCustom, calls=%fused_computation.26 | custom fusion | flops 851968 | bytes 1049088 | tf_op jit(solution)/shard_map/scatter-add | solution.py:85
  629.4 6.2 convolution_bitcast_fusion
  635.6 5.1 fusion.6
  640.7 4.2 fusion.3
  644.8 67.5 %all-reduce.2 = f32[3456]{0:T(1024)} all-reduce(f32[3456]{0:T(1024)S(1)} %fusion.3), channel_id=4, replica_groups=mesh['dp'=32,'rep'=4] {'dp','rep'}, use_global_device_ids=true, to_apply=%region_14.15.clone | all-reduce | flops 3456 | bytes 27648
  716.5 3.0 divide_subtract_fusion
  719.4 140.0 %all-reduce.9.cloned.1.call-done = (f32[1024,128]{1,0:T(8,128)}, f32[512,3456]{1,0:T(8,128)}, f32[3456,512]{0,1:T(8,128)}) async-done(((f32[1024,128]{1,0:T(8,128)}, f32[512,3456]{1,0:T(8,128)}, f32[3456,512]{0,1:T(8,128)}), (f32[1024,128]{1,0:T(8,128)}, f32[512,3456]{1,0:T(8,128)}, f32[3456,512]{0,1:T(8,128)})) %all-reduce.9.cloned.1.call-update) | async-done | bytes 14680080 | tf_op jit(solution)/shard_map/psum | solution.py:90
  865.5 2.2 divide_subtract_fusion.1
  (69 shorter events, 49.2 us)
Async XLA Ops:
  7.2 362.8 %copy-start = (bf16[512,3456]{1,0:T(8,128)(2,1)S(1)}, bf16[512,3456]{1,0:T(8,128)(2,1)}, u32[]{:S(2)}) copy-start(bf16[512,3456]{1,0:T(8,128)(2,1)} %param.13) | copy-start | bytes 10616836
  16.4 0.6 copy-start.2
  353.9 144.3 %all-to-all-start = ((s32[32,1,208]{2,1,0:T(1,128)}), s32[32,1,208]{2,1,0:T(1,128)}, u32[]{:S(2)}, u32[]{:S(2)}) async-start(s32[32,1,208]{2,1,0:T(1,128)} %all_to_all.9), calls=%async_computation | async-start | bytes 65536 | tf_op jit(solution)/shard_map/all_to_all | solution.py:83
  363.7 3.1 copy-start.3
  363.7 4.1 copy-start.7
  367.9 2.1 copy-start.5
  369.9 2.1 copy-start.9
  372.1 4.3 copy-start.11
  372.1 2.2 copy-start.8
  374.3 2.1 copy-start.12
  498.2 131.1 %copy-start.4 = (bf16[512,3456]{1,0:T(8,128)(2,1)S(1)}, bf16[512,3456]{1,0:T(8,128)(2,1)}, u32[]{:S(2)}) copy-start(bf16[512,3456]{1,0:T(8,128)(2,1)} %param.10) | copy-start | bytes 10616836
  498.2 90.0 %all-to-all-start.1 = ((f32[32,208,128]{2,1,0:T(8,128)}), f32[32,208,128]{2,1,0:T(8,128)}, u32[]{:S(2)}, u32[]{:S(2)}) async-start(f32[32,208,128]{2,1,0:T(8,128)} %bitcast.56), calls=%async_computation.1 | async-start | bytes 6815744 | tf_op jit(solution)/shard_map/all_to_all | solution.py:82
  506.1 207.5 %all-reduce.7.cloned.1.call-start = ((), (), s32[]{:S(2)}) async-start(), calls=%async_computation.2 | async-start | bytes 2097152 | tf_op jit(solution)/shard_map/psum | solution.py:88
  629.3 230.1 %all-reduce.9.cloned.1.call-start = ((), (), s32[]{:S(2)}) async-start(), calls=%async_computation.3 | async-start | bytes 29360128 | tf_op jit(solution)/shard_map/psum | solution.py:90
  629.3 6.2 copy-start.6
  629.4 6.2 copy-start.10
  640.7 228.6 %copy-start.1 = (bf16[512,3456]{1,0:T(8,128)(2,1)S(1)}, bf16[512,3456]{1,0:T(8,128)(2,1)}, u32[]{:S(2)}) copy-start(bf16[512,3456]{1,0:T(8,128)(2,1)} %param.13) | copy-start | bytes 10616836
Sparse Core Ops, SparseCore 0:
  629.4 46.4 all-reduce.6
  683.0 176.4 all-reduce.8
where the time goes:
time: 884 us; the launch traced here: 876 us
  local copies, waits for them, and re-layouts  435 us (49%)
  other arithmetic  182 us (21%)
  waiting for transfers between devices  140 us (16%)
  blocking collectives  67.5 us (8%)
  matrix products  19.6 us (2%)
  starting transfers between devices  17.8 us (2%)
  between operations  14.5 us (2%)
    psum x1, waiting for transfers between devices, body(): freq_total = lax.psum(freq_grad, ('dp', 'rep'))  140 us
    gather x1, local copies, waits for them, and re-layouts, body(): sorted_owner = owners[sorted_order]  121 us
    gather x1, local copies, waits for them, and re-layouts, body(): owner_row[sorted_order]  121 us
    scatter x1, local copies, waits for them, and re-layouts, body(): bucket = jnp.zeros((shards * capacity + 1, emb_width), jnp.float32).at[ta...  109 us
    scatter-add x1, other arithmetic, body(): jax.ops.segment_sum(values, jnp.where(is_frequent, places, f_count), f_co...  72.4 us
    unnamed x1, blocking collectives  67.5 us
    scatter x1, local copies, waits for them, and re-layouts, body(): jnp.zeros((shards * capacity + 1,), jnp.int32).at[target]  49.8 us
    scatter-add x1, other arithmetic, body(): jax.ops.segment_sum(arrived.reshape(-1, emb_width), arrived_rows.reshape(...  41 us
  transfers between devices with their start and end apart: 4, of which 1 were waited for; matrix products, arithmetic and copies ran while one was open for 27% of the time, Pallas kernels for 0%

commit v1 on v0

--- a/solution.py
+++ b/solution.py
@@ -87,7 +87,7 @@
     )
     shard_grad = lax.psum(shard_grad, "rep")
     new_shard, new_shard_accum = row_adagrad(shard_table, shard_accum, shard_grad)
-    freq_total = lax.psum(freq_grad, ("dp", "rep"))
+    freq_total = jnp.sum(lax.all_gather(freq_grad, ("dp", "rep")), axis=0)
     new_frequent, new_frequent_accum = row_adagrad(frequent_table, frequent_accum, freq_total)
     return (
         new_frequent,

time: 884 us -> 1030 us (1.17)
  waiting for transfers between devices: 140 us -> 262 us
  other arithmetic: 182 us -> 202 us
    all_gather x0 -> x1, waiting for transfers between devices: none -> 163 us  [body(): freq_total = jnp.sum(lax.all_gather(freq_grad, ('dp', 'rep')), axis=0)]
    psum x1 -> x0, waiting for transfers between devices: 140 us -> none  [body(): freq_total = lax.psum(freq_grad, ('dp', 'rep'))]
    unnamed x2 -> x4, waiting for transfers between devices: 0.03 us -> 59.2 us
    all_to_all x1, waiting for transfers between devices: 0.01 us -> 39.8 us  [body(): lax.all_to_all(bucket, 'dp', split_axis=0, concat_axis=0, tiled=True)]
    reduce_sum x0 -> x1, other arithmetic: none -> 21.8 us  [body(): freq_total = jnp.sum(lax.all_gather(freq_grad, ('dp', 'rep')), axis=0)]
  transfers between devices with their start and end apart: 4 -> 5, of which waited for: 1 -> 3; matrix products, arithmetic and copies ran while one was open for 27% -> 24% of each run, Pallas kernels for 0% -> 0%
where the time goes in v1:
time: 1030 us; the launch traced here: 1020 us
  local copies, waits for them, and re-layouts  436 us (42%)
  waiting for transfers between devices  262 us (25%)
  other arithmetic  202 us (20%)
  blocking collectives  66.6 us (6%)
  matrix products  19.7 us (2%)
  starting transfers between devices  17.6 us (2%)
  between operations  14.2 us (1%)
    all_gather x1, waiting for transfers between devices, body(): freq_total = jnp.sum(lax.all_gather(freq_grad, ('dp', 'rep')), axis=0)  163 us
    gather x1, local copies, waits for them, and re-layouts, body(): sorted_owner = owners[sorted_order]  121 us
    gather x1, local copies, waits for them, and re-layouts, body(): owner_row[sorted_order]  121 us
    scatter x1, local copies, waits for them, and re-layouts, body(): bucket = jnp.zeros((shards * capacity + 1, emb_width), jnp.float32).at[ta...  110 us
    scatter-add x1, other arithmetic, body(): jax.ops.segment_sum(values, jnp.where(is_frequent, places, f_count), f_co...  72.2 us
    unnamed x1, blocking collectives  66.6 us
    unnamed x4, waiting for transfers between devices  59.2 us
    scatter x1, local copies, waits for them, and re-layouts, body(): jnp.zeros((shards * capacity + 1,), jnp.int32).at[target]  49.8 us
  transfers between devices with their start and end apart: 5, of which 3 were waited for; matrix products, arithmetic and copies ran while one was open for 24% of the time, Pallas kernels for 0%

profile of v1, /device:TPU:1, one launch (start us, length us, event | category | flops | bytes accessed | tf_op | source)
XLA Modules:
  0.0 1018.0 jit_solution(5747077863481671862)
XLA Ops:
  22.4 9.1 sort.17
  32.9 121.2 %gather_fusion = s32[13312]{0:T(1024)} fusion(s32[13312]{0:T(1024)} %copy-done.2, s32[13312]{0:T(1024)} %fusion.19), kind=kCustom, calls=%fused_computation | custom fusion | bytes 159744 | tf_op jit(solution)/shard_map/gather | solution.py:66
  154.1 5.3 compare_select_fusion.3
  159.4 4.2 compare_reduce_fusion.25
  163.7 16.6 %select_select_fusion = s32[13312]{0:T(1024)S(1)} fusion(pred[13312]{0:T(1024)(128)(4,1)S(1)} %get-tuple-element.62, pred[13312]{0:T(1024)(128)(4,1)S(1)} %get-tuple-element.61, pred[13312]{0:T(1024)(128)(4,1)S(1)} %get-tuple-element.60, pred[13312]{0:T(1024)(128)(4,1)S(1)} %get-tuple-element.59, pred[13312]{0:T(1024)(128)(4,1)S(1)} %get-tuple-element.58, ...), kind=kLoop, calls=%fused_computation.77 | loop fusion | flops 346112 | bytes 452712 | tf_op jit(solution)/shard_map/gather | solution.py:69
  181.8 120.7 %gather_fusion.1 = s32[13312]{0:T(1024)} fusion(s32[13312]{0:T(1024)} %get-tuple-element.71, s32[13312]{0:T(1024)} %fusion.19), kind=kCustom, calls=%fused_computation.1 | custom fusion | bytes 159744 | tf_op jit(solution)/shard_map/gather | solution.py:78
  302.6 49.8 %scatter_custom_fusion.1 = s32[6657]{0:T(1024)} fusion(s32[13312]{0:T(1024)} %bitcast.63, s32[13312]{0:T(1024)} %gather_fusion.1, s32[]{:T(128)} %constant.29.clone.1), kind=kCustom, calls=%fused_computation.83 | custom fusion | bytes 27140 | tf_op jit(solution)/shard_map/scatter | solution.py:78
  353.9 9.8 all-to-all-start
  376.5 3.3 slice_add_fusion
  379.8 7.8 reshape.231
  387.6 109.8 %scatter_custom_fusion.2 = f32[6657,128]{1,0:T(8,128)} fusion(s32[13312]{0:T(1024)} %bitcast.64, f32[13312,128]{1,0:T(8,128)} %reshape.231, s32[13312]{0:T(1024)} %fusion.19, f32[]{:T(128)} %constant.21.clone.1), kind=kCustom, calls=%fused_computation.12 | custom fusion | bytes 3408896 | tf_op jit(solution)/shard_map/scatter | solution.py:74
  497.4 4.2 slice.62
  501.5 7.6 all-to-all-start.1
  512.1 39.8 %all-to-all-done.1 = f32[32,208,128]{2,1,0:T(8,128)} async-done(((f32[32,208,128]{2,1,0:T(8,128)}), f32[32,208,128]{2,1,0:T(8,128)}, u32[]{:S(2)}, u32[]{:S(2)}) %all-to-all-start.1) | async-done | bytes 3407904 | tf_op jit(solution)/shard_map/all_to_all | solution.py:82
  551.8 41.2 %scatter_custom_fusion.3 = f32[2048,128]{1,0:T(8,128)} fusion(s32[6656]{0:T(1024)} %reshape.253, f32[6656,128]{1,0:T(8,128)} %bitcast.41, f32[]{:T(128)} %constant.21.clone.1), kind=kCustom, calls=%fused_computation.26 | custom fusion | flops 851968 | bytes 1049088 | tf_op jit(solution)/shard_map/scatter-add | solution.py:85
  593.2 6.2 convolution_bitcast_fusion
  599.4 5.0 fusion.6
  609.4 72.2 %scatter_custom_fusion = f32[1025,128]{1,0:T(8,128)} fusion(s32[13312]{0:T(1024)} %bitcast.65, f32[13312,128]{1,0:T(8,128)} %reshape.231, f32[]{:T(128)} %constant.21.clone.1), kind=kCustom, calls=%fused_computation.33 | custom fusion | flops 1703936 | bytes 525312 | tf_op jit(solution)/shard_map/scatter-add | solution.py:58
  683.5 3.0 fusion.3
  686.6 66.6 %all-reduce.2 = f32[3456]{0:T(1024)S(1)} all-reduce(f32[3456]{0:T(1024)S(1)} %fusion.3), channel_id=5, replica_groups=mesh['dp'=32,'rep'=4] {'dp','rep'}, use_global_device_ids=true, to_apply=%region_14.15.clone | all-reduce | flops 3456 | bytes 27648
  756.6 2.9 divide_subtract_fusion
  759.4 59.1 %all-reduce.9.cloned.1.call-done = (f32[512,3456]{1,0:T(8,128)}, f32[3456,512]{0,1:T(8,128)}) async-done(((f32[512,3456]{1,0:T(8,128)}, f32[3456,512]{0,1:T(8,128)}), (f32[512,3456]{1,0:T(8,128)}, f32[3456,512]{0,1:T(8,128)})) %all-reduce.9.cloned.1.call-update) | async-done | bytes 14155792
  822.1 163.3 %all-gather.3.cloned.1.call-done = f32[131072,128]{1,0:T(8,128)} async-done(((f32[1024,128]{1,0:T(8,128)}), f32[131072,128]{1,0:T(8,128)}) %all-gather.3.cloned.1.call-update) | async-done | bytes 67108880 | tf_op jit(solution)/shard_map/all_gather | solution.py:90
  985.4 21.8 %reduce_sum.45 = f32[1024,128]{1,0:T(8,128)} reduce(f32[128,1024,128]{2,1,0:T(8,128)} %bitcast.1, f32[]{:T(128)} %constant.21.clone.1), dimensions={0}, to_apply=%region_1.0 | reduce | flops 16646144 | bytes 67633152 | tf_op jit(solution)/shard_map/reduce_sum | solution.py:90
  (73 shorter events, 53.3 us)
Async XLA Ops:
  7.2 362.8 %copy-start = (bf16[512,3456]{1,0:T(8,128)(2,1)S(1)}, bf16[512,3456]{1,0:T(8,128)(2,1)}, u32[]{:S(2)}) copy-start(bf16[512,3456]{1,0:T(8,128)(2,1)} %param.13) | copy-start | bytes 10616836
  16.4 0.6 copy-start.2
  353.9 147.7 %all-to-all-start = ((s32[32,1,208]{2,1,0:T(1,128)}), s32[32,1,208]{2,1,0:T(1,128)}, u32[]{:S(2)}, u32[]{:S(2)}) async-start(s32[32,1,208]{2,1,0:T(1,128)} %all_to_all.9), calls=%async_computation | async-start | bytes 65536 | tf_op jit(solution)/shard_map/all_to_all | solution.py:83
  363.7 3.1 copy-start.3
  363.7 4.1 copy-start.7
  367.9 2.1 copy-start.5
  370.0 2.3 copy-start.8
  372.2 4.2 copy-start.10
  374.3 2.2 copy-start.11
  497.4 95.8 %copy-start.4 = (bf16[512,3456]{1,0:T(8,128)(2,1)S(1)}, bf16[512,3456]{1,0:T(8,128)(2,1)}, u32[]{:S(2)}) copy-start(bf16[512,3456]{1,0:T(8,128)(2,1)} %param.10) | copy-start | bytes 10616836
  501.5 50.3 %all-to-all-start.1 = ((f32[32,208,128]{2,1,0:T(8,128)}), f32[32,208,128]{2,1,0:T(8,128)}, u32[]{:S(2)}, u32[]{:S(2)}) async-start(f32[32,208,128]{2,1,0:T(8,128)} %bitcast.57), calls=%async_computation.1 | async-start | bytes 6815744 | tf_op jit(solution)/shard_map/all_to_all | solution.py:82
  509.1 244.6 %all-reduce.7.cloned.1.call-start = ((), (), s32[]{:S(2)}) async-start(), calls=%async_computation.2 | async-start | bytes 2097152 | tf_op jit(solution)/shard_map/psum | solution.py:88
  593.1 225.5 %all-reduce.9.cloned.1.call-start = ((), (), s32[]{:S(2)}) async-start(), calls=%async_computation.4 | async-start | bytes 28311552
  593.2 6.2 copy-start.6
  593.2 6.2 copy-start.9
  604.4 381.0 %all-gather.3.cloned.1.call-start = ((), (), s32[]{:S(2)}) async-start(), calls=%async_computation.3 | async-start | bytes 67633152 | tf_op jit(solution)/shard_map/all_gather | solution.py:90
  985.4 23.1 %copy-start.12 = (f32[1024]{0:T(1024)S(1)}, f32[1024]{0:T(1024)}, u32[]{:S(2)}) copy-start(f32[1024]{0:T(1024)} %param.17) | copy-start | bytes 12292
  985.4 25.9 %copy-start.1 = (bf16[512,3456]{1,0:T(8,128)(2,1)S(1)}, bf16[512,3456]{1,0:T(8,128)(2,1)}, u32[]{:S(2)}) copy-start(bf16[512,3456]{1,0:T(8,128)(2,1)} %param.13) | copy-start | bytes 10616836
Sparse Core Ops, SparseCore 0:
  593.2 45.0 all-reduce.6
  644.2 174.3 all-reduce.8
  822.3 162.9 all-gather.2
